TPU v7x, 32 devices: a whole 2x2x4 slice. The times are simulated.
32 devices in a mesh: groups: 2 (over y), row: 4 (over z), col: 4 (over x, core).
Axes of the slice: x: 2, y: 2, z: 4, core: 2. Of those that a mesh axis runs over, the one named last changes fastest.
Arguments:
- pair: bfloat16 [512, 16384], P(('groups', 'row'), 'col'), parts along dimension 0, may hold values from -6 to 6
- res_mask: int32 [512], P('groups'), parts along dimension 0, may hold values 0 or 1
- present: int32 [512], P('groups'), parts along dimension 0, may hold values 0 or 1
- ln_in_gain: float32 [64], replicated, may hold values from 0.1 to 1.9
- w_proj: bfloat16 [64, 256], replicated, may hold values from -0.75 to 0.75
- w_gate: bfloat16 [64, 64], replicated, may hold values from -0.75 to 0.75
- ln_out_gain: float32 [64], replicated, may hold values from 0.1 to 1.9
- w_out: bfloat16 [64, 64], replicated, may hold values from -0.75 to 0.75
Outputs:
- update: bfloat16 [512, 16384], P(('groups', 'row'), 'col'), parts along dimension 0
There are 2 independent parts, one for each index of `groups`. A program takes and returns all parts, laid end to end along the dimension named above; an argument that names none is the same for every part. Nothing has to cross between parts.
All inputs are finite; a program needn't handle non-finite values.
Results may differ from a plain program's by a relative error of at most 0.0078.
Values may be sent and summed in bfloat16 or wider, within the bound.
A program may use at most 64 MiB of HBM per device.

v0:
```python
import functools

import jax
import jax.numpy as jnp
from jax import lax
from jax.experimental import pallas as pl
from jax.experimental.pallas import tpu as pltpu
from jax.sharding import PartitionSpec as P

NT = (((1,), (1,)), ((), ()))
NN = (((1,), (0,)), ((), ()))
EIGHT = 8
LANES = 128
CHUNKS = 4


def dot(lhs, rhs, dims):
    return lax.dot_general(lhs, rhs, dims, preferred_element_type=jnp.float32)


def flipped(value, mask, count):
    total = 0
    step = 1
    while step < count:
        total = total + ((value // step + mask // step) % 2) * step
        step *= 2
    return total


def lane_pair(left, right, half):
    w = LANES // 2
    return jnp.concatenate(
        [left[:, half * w : (half + 1) * w], right[:, half * w : (half + 1) * w]], axis=1
    )


def iota(shape, dim):
    return lax.broadcasted_iota(jnp.int32, shape, dim)


def fused_kernel(
    R, C, pair_hbm, res_hbm, present_hbm, gain_in_hbm, w_proj_hbm, w_gate_hbm, gain_out_hbm,
    w_out_hbm, out_hbm, pair_ref, res_ref, present_ref, gain_in_ref, w_proj_ref, w_gate_ref,
    gain_out_ref, w_out_ref, out_ref, normed, gate, wide, masks, send1, recv1, send2, recv2,
    send_sem1, recv_sem1, send_sem2, recv_sem2, local_sem, in_sem, out_sem,
):
    f32, bf16 = jnp.float32, jnp.bfloat16
    rows = pair_ref.shape[0]
    chans = w_gate_ref.shape[0]
    hidden = w_out_ref.shape[0]
    ndev = R * C
    depth = R // 2
    team = depth * C
    own = hidden // team
    per = own // CHUNKS
    groups = normed.shape[0] // rows
    pairs = groups // 2
    block = EIGHT * chans
    half_block = block // 2
    r, c = lax.axis_index("row"), lax.axis_index("col")
    me = r * C + c
    half_row = r // depth * depth
    seat = r % depth * C + c

    def mate(n):
        row = half_row + flipped(r % depth, depth - 1 - n // C, depth)
        return row, flipped(c, C - 1 - n % C, C)

    def partner(n):
        return flipped(r, R - 1 - n // C, R), flipped(c, C - 1 - n % C, C)

    barrier = pltpu.get_barrier_semaphore()

    def greet(n, carry):
        pr, pc = partner(n)
        pl.semaphore_signal(
            barrier, inc=1, device_id={"row": pr, "col": pc}, device_id_type=pl.DeviceIdType.MESH
        )
        return carry

    lax.fori_loop(0, ndev - 1, greet, 0)
    loads = [
        pltpu.make_async_copy(source, target, in_sem.at[at])
        for at, (source, target) in enumerate(
            (
                (pair_hbm, pair_ref), (gain_in_hbm, gain_in_ref), (gain_out_hbm, gain_out_ref),
                (res_hbm, res_ref), (present_hbm, present_ref), (w_proj_hbm, w_proj_ref),
                (w_gate_hbm, w_gate_ref), (w_out_hbm, w_out_ref),
            )
        )
    ]
    for load in loads:
        load.start()
    for load in loads:
        load.wait()

    eye = iota((chans, chans), 0) == iota((chans, chans), 1)
    sub_id, lane_in = iota((chans, block), 0), iota((chans, block), 1)

    def over_lanes(gain_ref, match):
        column = jnp.sum(jnp.where(eye, gain_ref[...], 0.0), axis=1, keepdims=True)
        return jnp.sum(jnp.where(match, column, 0.0), axis=0, keepdims=True)

    gain_in = over_lanes(gain_in_ref, lane_in % chans == sub_id)
    gain_out = over_lanes(gain_out_ref, lane_in // EIGHT == sub_id)

    same = (iota((half_block, half_block), 0) // chans) == (
        iota((half_block, half_block), 1) // chans
    )
    ones = same.astype(f32).astype(bf16)
    for h in range(2):
        parts = []
        for qp in range(pairs):
            for par in range(2):
                lo = (par * pairs + qp) * block + h * half_block
                parts.append(pair_ref[:, lo : lo + half_block])
        x = jnp.concatenate(parts, axis=0)
        d = x.astype(f32) - dot(x, ones, NN) * (1.0 / chans)
        sq = d * d
        hi = sq.astype(bf16)
        lo_part = (sq - hi.astype(f32)).astype(bf16)
        var = (dot(hi, ones, NN) + dot(lo_part, ones, NN)) * (1.0 / chans)
        y = d * lax.rsqrt(var + 1e-05) * gain_in[:, h * half_block : (h + 1) * half_block]
        normed[:, h * half_block : (h + 1) * half_block] = y.astype(bf16)

    count = res_ref.shape[1]
    alive = (res_ref[...] * present_ref[...]).astype(f32)
    wide_lanes = groups * rows
    res_id, lane = iota((count, wide_lanes), 0), iota((count, wide_lanes), 1)
    group = (lane // rows) % 2 * pairs + lane // LANES
    is_row = (res_id == r * rows + lane % rows).astype(f32).astype(bf16)
    is_col = (res_id // EIGHT == c * groups + group).astype(f32).astype(bf16)
    shape = (per * EIGHT, count)
    phase = iota(shape, 0) % EIGHT == iota(shape, 1) % EIGHT
    rows_alive = dot(jnp.broadcast_to(alive, shape).astype(bf16), is_row, NN)
    masks[...] = rows_alive * dot(jnp.where(phase, alive, 0.0).astype(bf16), is_col, NN)

    stacked = jnp.concatenate([w_proj_ref[...]] * EIGHT, axis=0)
    part = per * EIGHT
    n_rows = team * 4 * part
    out_chans = w_proj_ref.shape[1]
    diag = (iota((n_rows, block), 0) % EIGHT) == (iota((n_rows, block), 1) // chans)
    row_id = iota((n_rows, out_chans), 0)
    target = row_id // part % 4 * hidden + row_id // (4 * part) * own + row_id % part // EIGHT
    target = iota((n_rows, out_chans), 1) - target

    def project(h):
        pick = (target == h * per).astype(f32).astype(bf16)
        weights = jnp.where(diag, dot(pick, stacked, NT), 0.0).astype(bf16)
        res = dot(weights, normed[...], NT)
        mask = masks[...]
        for dest in range(team):
            for which in range(2):
                lo = (4 * dest + 2 * which) * part
                g, v = res[lo : lo + part], res[lo + part : lo + 2 * part]
                val = mask * jax.nn.sigmoid(g) * v
                for ch in range(per):
                    tile = jnp.concatenate(
                        [
                            val[ch * EIGHT : (ch + 1) * EIGHT, qp * LANES : (qp + 1) * LANES]
                            for qp in range(pairs)
                        ],
                        axis=0,
                    )
                    send1[h, dest, ch, which] = tile.astype(bf16)

    def remote(source, target, ssem, rsem, where):
        return pltpu.make_async_remote_copy(
            src_ref=source, dst_ref=target, send_sem=ssem, recv_sem=rsem,
            device_id={"row": where[0], "col": where[1]}, device_id_type=pl.DeviceIdType.MESH,
        )

    def copy1(h, n, sending):
        where = mate(n)
        p = (where[0] - half_row) * C + where[1]
        at = seat if sending else p
        return remote(
            send1.at[h, p], recv1.at[h, at], send_sem1.at[h, p], recv_sem1.at[h, at], where
        )

    def copy2(piece, n, sending):
        where = partner(n)
        p = where[0] * C + where[1]
        at = me if sending else p
        last = CHUNKS - 1
        key = (lambda d: (piece, d)) if piece < last else (lambda d: (last, d, piece - last))
        return remote(
            send2.at[key(p)], recv2.at[key(at)],
            send_sem2.at[piece, p], recv_sem2.at[piece, at], where,
        )

    def each(total, body):
        def run(n, carry):
            body(n)
            return carry

        lax.fori_loop(0, total - 1, run, 0)

    gate_rows = jnp.concatenate([w_gate_ref[...]] * (half_block // chans), axis=0)
    spread = ((iota((chans, block), 1) % chans) == iota((chans, block), 0)).astype(f32).astype(bf16)
    w_gate4 = jnp.where(same, dot(gate_rows, spread[:, :half_block], NN), 0.0).astype(bf16)

    def output_gate(h):
        cols = slice(h * half_block, (h + 1) * half_block)
        gate[:, cols] = jax.nn.sigmoid(dot(normed[:, cols], w_gate4, NN))

    own1 = [
        pltpu.make_async_copy(send1.at[h, seat], recv1.at[h, seat], local_sem.at[h])
        for h in range(CHUNKS)
    ]
    tiled = dot(w_out_ref[...], spread, NN).astype(bf16)
    big = hidden * EIGHT
    pick_out = ((iota((big, hidden), 0) // EIGHT) == iota((big, hidden), 1)).astype(f32).astype(bf16)
    diag_out = (iota((big, block), 0) % EIGHT) == (iota((big, block), 1) // chans)

    sub = pairs * EIGHT

    def multiply(h, ch):
        full = []
        for which in range(2):
            by_parity = [[], []]
            for rp in range(depth // 2):
                one, two = (
                    jnp.concatenate(
                        [recv1[h, (2 * rp + e) * C + cc, ch, which] for cc in range(C)], axis=0
                    ).astype(f32)
                    for e in range(2)
                )
                for par in range(2):
                    by_parity[par].append(lane_pair(one, two, par).astype(bf16))
            full.append([jnp.concatenate(p, axis=1) for p in by_parity])
        a_rows = jnp.concatenate(
            [full[0][par][cc * sub : (cc + 1) * sub] for cc in range(C) for par in range(2)], axis=0
        )
        even, odd = (dot(full[1][par], a_rows, NT) for par in range(2))
        for rp in range(R // 2):
            cols = slice(rp * LANES, (rp + 1) * LANES)
            for e in range(2):
                tile = lane_pair(even[:, cols], odd[:, cols], e).astype(bf16)
                for cc in range(C):
                    for two in range(2):
                        lo = cc * sub + two * (sub // 2)
                        send2[h, (2 * rp + e) * C + cc, two, ch] = tile[lo : lo + sub // 2]

    own2 = [
        pltpu.make_async_copy(send2.at[h, me], recv2.at[h, me], local_sem.at[CHUNKS + h])
        for h in range(CHUNKS)
    ]
    def answer(h):
        own1[h].wait()
        each(team, lambda n, h=h: copy1(h, n, False).wait())
        for ch in range(per):
            multiply(h, ch)
        for piece in (h,) if h < CHUNKS - 1 else (h, h + 1):
            each(ndev, lambda n, piece=piece: copy2(piece, n, True).start())
        own2[h].start()

    for h in range(CHUNKS):
        project(h)
        if h == 0:
            pl.semaphore_wait(barrier, ndev - 1)
        if h in (1, 2):
            output_gate(h - 1)
        each(team, lambda n, h=h: copy1(h, n, True).start())
        own1[h].start()
        if h >= 2:
            answer(h - 2)
    for h in range(max(CHUNKS - 2, 0), CHUNKS):
        answer(h)
    for h in range(max(CHUNKS, 1), 3):
        output_gate(h - 1)
    wide[...] = jnp.where(diag_out, dot(pick_out, tiled, NN), 0.0).astype(bf16)

    for copy in own2:
        copy.wait()
    for piece in range(CHUNKS - 1):
        each(ndev, lambda n, piece=piece: copy2(piece, n, False).wait())
    stores = []
    for two in range(pairs // 2):
        each(ndev, lambda n, two=two: copy2(CHUNKS - 1 + two, n, False).wait())
        t = jnp.concatenate(
            [
                (recv2[h, :team, two].astype(f32) + recv2[h, team:, two].astype(f32))[:, None]
                for h in range(CHUNKS)
            ],
            axis=1,
        ).reshape(hidden, 16, LANES)
        mean = jnp.sum(t, axis=0, keepdims=True) * (1.0 / hidden)
        d = t - mean
        var = jnp.sum(d * d, axis=0, keepdims=True) * (1.0 / hidden)
        y = d * lax.rsqrt(var + 1e-05)
        for e in range(2):
            qp = 2 * two + e
            flat = y[:, e * EIGHT : (e + 1) * EIGHT, :].reshape(big, LANES)
            lhs = (flat.T * gain_out).astype(bf16)
            res = dot(lhs, wide[...], NN)
            for par in range(2):
                g = gate[(2 * qp + par) * rows : (2 * qp + par + 1) * rows, :]
                val = g * res[par * rows : (par + 1) * rows]
                lo = (par * pairs + qp) * block
                out_ref[:, lo : lo + block] = val.astype(bf16)
                store = pltpu.make_async_copy(
                    out_ref.at[:, pl.ds(lo, block)], out_hbm.at[:, pl.ds(lo, block)],
                    out_sem.at[len(stores)],
                )
                store.start()
                stores.append(store)
    for store in stores:
        store.wait()


def fused(pair, res_mask, present, ln_in_gain, w_proj, w_gate, ln_out_gain, w_out):
    R, C = lax.axis_size("row"), lax.axis_size("col")
    rows, width = pair.shape
    chans, hidden = w_gate.shape[0], w_out.shape[0]
    cols = width // chans
    groups = cols // EIGHT
    pairs = groups // 2
    ndev = R * C
    team = ndev // 2
    own = hidden // team
    per = own // CHUNKS
    bf16 = jnp.bfloat16
    anywhere = pl.BlockSpec(memory_space=pl.ANY)
    operands = (
        pair, res_mask[None, :], present[None, :], ln_in_gain[None, :], w_proj, w_gate,
        ln_out_gain[None, :], w_out,
    )
    sub = pairs * EIGHT
    return pl.pallas_call(
        functools.partial(fused_kernel, R, C),
        out_shape=jax.ShapeDtypeStruct(pair.shape, bf16),
        in_specs=[anywhere] * len(operands),
        out_specs=anywhere,
        scratch_shapes=[pltpu.VMEM(value.shape, value.dtype) for value in operands]
        + [
            pltpu.VMEM(pair.shape, bf16),
            pltpu.VMEM((groups * rows, EIGHT * chans), bf16),
            pltpu.VMEM((groups * rows, EIGHT * chans), jnp.float32),
            pltpu.VMEM((hidden * EIGHT, EIGHT * chans), bf16),
            pltpu.VMEM((per * EIGHT, groups * rows), jnp.float32),
            pltpu.VMEM((CHUNKS, team, per, 2, sub, LANES), bf16),
            pltpu.VMEM((CHUNKS, team, per, 2, sub, LANES), bf16),
            pltpu.VMEM((CHUNKS, ndev, 2, per, sub // 2, LANES), bf16),
            pltpu.VMEM((CHUNKS, ndev, 2, per, sub // 2, LANES), bf16),
            pltpu.SemaphoreType.DMA((CHUNKS, team)),
            pltpu.SemaphoreType.DMA((CHUNKS, team)),
            pltpu.SemaphoreType.DMA((CHUNKS + 1, ndev)),
            pltpu.SemaphoreType.DMA((CHUNKS + 1, ndev)),
            pltpu.SemaphoreType.DMA((2 * CHUNKS,)),
            pltpu.SemaphoreType.DMA((len(operands),)),
            pltpu.SemaphoreType.DMA((groups,)),
        ],
        compiler_params=pltpu.CompilerParams(collective_id=0, has_side_effects=True),
    )(*operands)


def fits(R, C, rows, cols, chans, hidden):
    powers = all(n & (n - 1) == 0 for n in (R, C))
    return (
        powers
        and R == C
        and R % 4 == 0
        and rows == cols == LANES // 2
        and chans == hidden == LANES // 2
        and hidden % (R * C // 2 * CHUNKS) == 0
    )


def swapped(value, axis, bit):
    mask = 2**bit
    pairs = [(source, source ^ mask) for source in range(lax.axis_size(axis))]
    return lax.ppermute(value, axis, pairs)


def layer_norm(values, gain):
    mean = jnp.mean(values, axis=-1, keepdims=True)
    var = jnp.mean((values - mean) ** 2, axis=-1, keepdims=True)
    return (values - mean) * lax.rsqrt(var + 1e-05) * gain


def local(pair, res_mask, present, ln_in_gain, w_proj, w_gate, ln_out_gain, w_out):
    rows_here, width = pair.shape
    chans = w_gate.shape[0]
    hidden = w_out.shape[0]
    cols_here = width // chans
    row_count = lax.axis_size("row")
    col_count = lax.axis_size("col")
    if fits(row_count, col_count, rows_here, cols_here, chans, hidden):
        return fused(pair, res_mask, present, ln_in_gain, w_proj, w_gate, ln_out_gain, w_out)
    row_index = lax.axis_index("row")
    col_index = lax.axis_index("col")
    z_tile = pair.astype(jnp.float32).reshape(rows_here, cols_here, chans)
    normed = (
        layer_norm(z_tile, ln_in_gain).astype(jnp.bfloat16).reshape(rows_here * cols_here, chans)
    )
    proj = jnp.dot(normed, w_proj, preferred_element_type=jnp.float32).reshape(
        rows_here, cols_here, 4 * hidden
    )
    weight = (res_mask * present).astype(jnp.float32)
    weight_rows = lax.dynamic_slice_in_dim(weight, row_index * rows_here, rows_here)
    weight_cols = lax.dynamic_slice_in_dim(weight, col_index * cols_here, cols_here)
    pair_mask = (weight_rows[:, None] * weight_cols[None, :])[:, :, None]
    a_tile = (
        pair_mask * jax.nn.sigmoid(proj[:, :, :hidden]) * proj[:, :, hidden : 2 * hidden]
    ).astype(jnp.bfloat16)
    b_tile = (
        pair_mask * jax.nn.sigmoid(proj[:, :, 2 * hidden : 3 * hidden]) * proj[:, :, 3 * hidden :]
    ).astype(jnp.bfloat16)
    gate = jax.nn.sigmoid(jnp.dot(normed, w_gate, preferred_element_type=jnp.float32)).reshape(
        rows_here, cols_here, chans
    )
    factor = 2 if row_count == 4 * col_count else 1
    square_rows = factor * rows_here
    wide_rows = lax.all_gather(a_tile, "col", axis=1, tiled=True)
    spread = wide_rows.reshape(rows_here, row_count // factor, 1, square_rows, hidden)
    spread = jnp.repeat(spread, factor, axis=2).reshape(rows_here, row_count * square_rows, hidden)
    a_square = lax.all_to_all(spread, "row", split_axis=1, concat_axis=0, tiled=True)
    copies = jnp.tile(b_tile, (1, row_count // factor, 1))
    b_square = lax.all_to_all(copies, "row", split_axis=1, concat_axis=0, tiled=True)
    tri_square = jnp.einsum("kic,kjc->ijc", a_square, b_square, preferred_element_type=jnp.float32)
    normed_square = layer_norm(tri_square, ln_out_gain).astype(jnp.bfloat16)
    if factor == 1:
        tri_norm = normed_square
    else:
        parity = row_index % 2
        own_part = lax.dynamic_slice_in_dim(normed_square, parity * rows_here, rows_here, 0)
        other_part = lax.dynamic_slice_in_dim(normed_square, (1 - parity) * rows_here, rows_here, 0)
        received = swapped(other_part, "row", 0)
        tri_norm = jnp.where(
            parity == 0,
            jnp.concatenate([own_part, received], axis=1),
            jnp.concatenate([received, own_part], axis=1),
        )
    flat_norm = tri_norm.reshape(rows_here * cols_here, hidden)
    projected = jnp.dot(flat_norm, w_out, preferred_element_type=jnp.float32).reshape(
        rows_here, cols_here, chans
    )
    return (gate * projected).astype(jnp.bfloat16).reshape(rows_here, cols_here * chans)


def solution(mesh):
    in_specs = (P(("groups", "row"), "col"), P("groups"), P("groups"), P(), P(), P(), P(), P())
    out_specs = P(("groups", "row"), "col")
    return jax.shard_map(local, mesh=mesh, in_specs=in_specs, out_specs=out_specs, check_vma=False)
```

profile of v0, /device:TPU:0, one launch (start us, length us, event | category | flops | bytes accessed | tf_op | source)
XLA Modules:
  0.0 42.2 jit_solution(15956721092988520018)
XLA Ops:
  0.0 40.4 %shard_map.82 = bf16[64,4096]{1,0:T(8,128)(2,1)} custom-call(bf16[64,4096]{1,0:T(8,128)(2,1)} %pair_hbm.1, s32[1,256]{1,0:T(1,128)} %bitcast.4, s32[1,256]{1,0:T(1,128)} %bitcast.5, f32[1,64]{1,0:T(1,128)} %bitcast.6, bf16[64,256]{1,0:T(8,128)(2,1)} %w_proj_hbm.1, bf16[64,64]{1,0:T(8,128)(2,1)} %w_gate_hbm.1, f32[1,64]{1,0:T(1,128)} %bitcast.7, ...), custom_call_target="tpu_custom_call" | custom-call | tf_op jit(solution)/shard_map/pallas_call | solution.py:330
  40.4 1.9 %copy.10 = bf16[64,4096]{1,0:T(8,128)(2,1)} copy(bf16[64,4096]{1,0:T(8,128)(2,1)} %shard_map.82) | data formatting | bytes 1048576
where the time goes:
time: 42.4 us; the launch traced here: 42.2 us
  Pallas kernels  40.4 us (95%)
  local copies, waits for them, and re-layouts  1.87 us (4%)
    pallas_call x1, Pallas kernels, fused(): pl.pallas_call(functools.partial(fused_kernel, R, C), out_shape=jax.Shape...  40.4 us
    unnamed x1, local copies, waits for them, and re-layouts  1.87 us

commit v1 on v0

--- a/solution.py
+++ b/solution.py
@@ -42,7 +42,7 @@
     R, C, pair_hbm, res_hbm, present_hbm, gain_in_hbm, w_proj_hbm, w_gate_hbm, gain_out_hbm,
     w_out_hbm, out_hbm, pair_ref, res_ref, present_ref, gain_in_ref, w_proj_ref, w_gate_ref,
     gain_out_ref, w_out_ref, out_ref, normed, gate, wide, masks, send1, recv1, send2, recv2,
-    send_sem1, recv_sem1, send_sem2, recv_sem2, local_sem, in_sem, out_sem,
+    send_sem1, recv_sem1, send_sem2, recv_sem2, in_sem, out_sem,
 ):
     f32, bf16 = jnp.float32, jnp.bfloat16
     rows = pair_ref.shape[0]
@@ -175,7 +175,7 @@
         p = (where[0] - half_row) * C + where[1]
         at = seat if sending else p
         return remote(
-            send1.at[h, p], recv1.at[h, at], send_sem1.at[h, p], recv_sem1.at[h, at], where
+            send1.at[h, p], recv1.at[h, at], send_sem1.at[0], recv_sem1.at[h], where
         )
 
     def copy2(piece, n, sending):
@@ -186,7 +186,7 @@
         key = (lambda d: (piece, d)) if piece < last else (lambda d: (last, d, piece - last))
         return remote(
             send2.at[key(p)], recv2.at[key(at)],
-            send_sem2.at[piece, p], recv_sem2.at[piece, at], where,
+            send_sem2.at[0], recv_sem2.at[piece], where,
         )
 
     def each(total, body):
@@ -205,9 +205,13 @@
         gate[:, cols] = jax.nn.sigmoid(dot(normed[:, cols], w_gate4, NN))
 
     own1 = [
-        pltpu.make_async_copy(send1.at[h, seat], recv1.at[h, seat], local_sem.at[h])
+        pltpu.make_async_copy(send1.at[h, seat], recv1.at[h, seat], recv_sem1.at[h])
         for h in range(CHUNKS)
     ]
+
+    def landed(ref, sem):
+        pltpu.make_async_copy(ref, ref, sem).wait()
+
     tiled = dot(w_out_ref[...], spread, NN).astype(bf16)
     big = hidden * EIGHT
     pick_out = ((iota((big, hidden), 0) // EIGHT) == iota((big, hidden), 1)).astype(f32).astype(bf16)
@@ -242,18 +246,21 @@
                         lo = cc * sub + two * (sub // 2)
                         send2[h, (2 * rp + e) * C + cc, two, ch] = tile[lo : lo + sub // 2]
 
-    own2 = [
-        pltpu.make_async_copy(send2.at[h, me], recv2.at[h, me], local_sem.at[CHUNKS + h])
-        for h in range(CHUNKS)
-    ]
+    def own2(piece):
+        if piece < CHUNKS - 1:
+            source, target = send2.at[piece, me], recv2.at[piece, me]
+        else:
+            half = piece - CHUNKS + 1
+            source, target = send2.at[CHUNKS - 1, me, half], recv2.at[CHUNKS - 1, me, half]
+        return pltpu.make_async_copy(source, target, recv_sem2.at[piece])
+
     def answer(h):
-        own1[h].wait()
-        each(team, lambda n, h=h: copy1(h, n, False).wait())
+        landed(recv1.at[h], recv_sem1.at[h])
         for ch in range(per):
             multiply(h, ch)
         for piece in (h,) if h < CHUNKS - 1 else (h, h + 1):
             each(ndev, lambda n, piece=piece: copy2(piece, n, True).start())
-        own2[h].start()
+            own2(piece).start()
 
     for h in range(CHUNKS):
         project(h)
@@ -271,13 +278,10 @@
         output_gate(h - 1)
     wide[...] = jnp.where(diag_out, dot(pick_out, tiled, NN), 0.0).astype(bf16)
 
-    for copy in own2:
-        copy.wait()
     for piece in range(CHUNKS - 1):
-        each(ndev, lambda n, piece=piece: copy2(piece, n, False).wait())
-    stores = []
+        landed(recv2.at[piece], recv_sem2.at[piece])
     for two in range(pairs // 2):
-        each(ndev, lambda n, two=two: copy2(CHUNKS - 1 + two, n, False).wait())
+        landed(recv2.at[CHUNKS - 1, :, two], recv_sem2.at[CHUNKS - 1 + two])
         t = jnp.concatenate(
             [
                 (recv2[h, :team, two].astype(f32) + recv2[h, team:, two].astype(f32))[:, None]
@@ -299,14 +303,12 @@
                 val = g * res[par * rows : (par + 1) * rows]
                 lo = (par * pairs + qp) * block
                 out_ref[:, lo : lo + block] = val.astype(bf16)
-                store = pltpu.make_async_copy(
-                    out_ref.at[:, pl.ds(lo, block)], out_hbm.at[:, pl.ds(lo, block)],
-                    out_sem.at[len(stores)],
-                )
-                store.start()
-                stores.append(store)
-    for store in stores:
-        store.wait()
+                pltpu.make_async_copy(
+                    out_ref.at[:, pl.ds(lo, block)], out_hbm.at[:, pl.ds(lo, block)], out_sem
+                ).start()
+    landed(out_ref, out_sem)
+    landed(send1.at[:, pl.ds(0, team - 1)], send_sem1.at[0])
+    landed(send2.at[:, pl.ds(0, ndev - 1)], send_sem2.at[0])
 
 
 def fused(pair, res_mask, present, ln_in_gain, w_proj, w_gate, ln_out_gain, w_out):
@@ -343,13 +345,12 @@
             pltpu.VMEM((CHUNKS, team, per, 2, sub, LANES), bf16),
             pltpu.VMEM((CHUNKS, ndev, 2, per, sub // 2, LANES), bf16),
             pltpu.VMEM((CHUNKS, ndev, 2, per, sub // 2, LANES), bf16),
-            pltpu.SemaphoreType.DMA((CHUNKS, team)),
-            pltpu.SemaphoreType.DMA((CHUNKS, team)),
-            pltpu.SemaphoreType.DMA((CHUNKS + 1, ndev)),
-            pltpu.SemaphoreType.DMA((CHUNKS + 1, ndev)),
-            pltpu.SemaphoreType.DMA((2 * CHUNKS,)),
+            pltpu.SemaphoreType.DMA((1,)),
+            pltpu.SemaphoreType.DMA((CHUNKS,)),
+            pltpu.SemaphoreType.DMA((1,)),
+            pltpu.SemaphoreType.DMA((CHUNKS + 1,)),
             pltpu.SemaphoreType.DMA((len(operands),)),
-            pltpu.SemaphoreType.DMA((groups,)),
+            pltpu.SemaphoreType.DMA,
         ],
         compiler_params=pltpu.CompilerParams(collective_id=0, has_side_effects=True),
     )(*operands)

time: 42.4 us -> 40.1 us (0.946)
  Pallas kernels: 40.4 us -> 38 us
    pallas_call x1, Pallas kernels: 40.4 us -> 38 us  [fused(): pl.pallas_call(functools.partial(fused_kernel, R, C), out_shape=jax.Shape...]
where the time goes in v1:
time: 40.1 us; the launch traced here: 39.9 us
  Pallas kernels  38 us (95%)
  local copies, waits for them, and re-layouts  1.87 us (5%)
    pallas_call x1, Pallas kernels, fused(): pl.pallas_call(functools.partial(fused_kernel, R, C), out_shape=jax.Shape...  38 us
    unnamed x1, local copies, waits for them, and re-layouts  1.87 us

profile of v1, /device:TPU:0, one launch (start us, length us, event | category | flops | bytes accessed | tf_op | source)
XLA Modules:
  0.0 39.9 jit_solution(1806654887696056032)
XLA Ops:
  0.0 38.0 %shard_map.82 = bf16[64,4096]{1,0:T(8,128)(2,1)} custom-call(bf16[64,4096]{1,0:T(8,128)(2,1)} %pair_hbm.1, s32[1,256]{1,0:T(1,128)} %bitcast.4, s32[1,256]{1,0:T(1,128)} %bitcast.5, f32[1,64]{1,0:T(1,128)} %bitcast.6, bf16[64,256]{1,0:T(8,128)(2,1)} %w_proj_hbm.1, bf16[64,64]{1,0:T(8,128)(2,1)} %w_gate_hbm.1, f32[1,64]{1,0:T(1,128)} %bitcast.7, ...), custom_call_target="tpu_custom_call" | custom-call | tf_op jit(solution)/shard_map/pallas_call | solution.py:332
  38.1 1.9 %copy.10 = bf16[64,4096]{1,0:T(8,128)(2,1)} copy(bf16[64,4096]{1,0:T(8,128)(2,1)} %shard_map.82) | data formatting | bytes 1048576

commit v2 on v1

--- a/solution.py
+++ b/solution.py
@@ -12,6 +12,7 @@
 EIGHT = 8
 LANES = 128
 CHUNKS = 4
+WRITE_GRANT = 2**20
 
 
 def dot(lhs, rhs, dims):
@@ -40,9 +41,9 @@
 
 def fused_kernel(
     R, C, pair_hbm, res_hbm, present_hbm, gain_in_hbm, w_proj_hbm, w_gate_hbm, gain_out_hbm,
-    w_out_hbm, out_hbm, pair_ref, res_ref, present_ref, gain_in_ref, w_proj_ref, w_gate_ref,
-    gain_out_ref, w_out_ref, out_ref, normed, gate, wide, masks, send1, recv1, send2, recv2,
-    send_sem1, recv_sem1, send_sem2, recv_sem2, in_sem, out_sem,
+    w_out_hbm, out_ref, pair_ref, res_ref, present_ref, gain_in_ref, w_proj_ref, w_gate_ref,
+    gain_out_ref, w_out_ref, normed, gate, wide, masks, send1, recv1, send2, recv2,
+    send_sem1, recv_sem1, send_sem2, recv_sem2, in_sem,
 ):
     f32, bf16 = jnp.float32, jnp.bfloat16
     rows = pair_ref.shape[0]
@@ -303,12 +304,14 @@
                 val = g * res[par * rows : (par + 1) * rows]
                 lo = (par * pairs + qp) * block
                 out_ref[:, lo : lo + block] = val.astype(bf16)
-                pltpu.make_async_copy(
-                    out_ref.at[:, pl.ds(lo, block)], out_hbm.at[:, pl.ds(lo, block)], out_sem
-                ).start()
-    landed(out_ref, out_sem)
     landed(send1.at[:, pl.ds(0, team - 1)], send_sem1.at[0])
     landed(send2.at[:, pl.ds(0, ndev - 1)], send_sem2.at[0])
+
+
+def write_kernel(update_ref, out_hbm, sem):
+    store = pltpu.make_async_copy(update_ref, out_hbm, sem)
+    store.start()
+    store.wait()
 
 
 def fused(pair, res_mask, present, ln_in_gain, w_proj, w_gate, ln_out_gain, w_out):
@@ -329,14 +332,13 @@
         ln_out_gain[None, :], w_out,
     )
     sub = pairs * EIGHT
-    return pl.pallas_call(
+    update = pl.pallas_call(
         functools.partial(fused_kernel, R, C),
-        out_shape=jax.ShapeDtypeStruct(pair.shape, bf16),
+        out_shape=pltpu.VMEM(pair.shape, bf16),
         in_specs=[anywhere] * len(operands),
-        out_specs=anywhere,
+        out_specs=pl.BlockSpec(memory_space=pltpu.VMEM),
         scratch_shapes=[pltpu.VMEM(value.shape, value.dtype) for value in operands]
         + [
-            pltpu.VMEM(pair.shape, bf16),
             pltpu.VMEM((groups * rows, EIGHT * chans), bf16),
             pltpu.VMEM((groups * rows, EIGHT * chans), jnp.float32),
             pltpu.VMEM((hidden * EIGHT, EIGHT * chans), bf16),
@@ -350,10 +352,17 @@
             pltpu.SemaphoreType.DMA((1,)),
             pltpu.SemaphoreType.DMA((CHUNKS + 1,)),
             pltpu.SemaphoreType.DMA((len(operands),)),
-            pltpu.SemaphoreType.DMA,
         ],
         compiler_params=pltpu.CompilerParams(collective_id=0, has_side_effects=True),
     )(*operands)
+    return pl.pallas_call(
+        write_kernel,
+        out_shape=jax.ShapeDtypeStruct(pair.shape, bf16),
+        in_specs=[anywhere],
+        out_specs=anywhere,
+        scratch_shapes=[pltpu.SemaphoreType.DMA],
+        compiler_params=pltpu.CompilerParams(vmem_limit_bytes=WRITE_GRANT),
+    )(update)
 
 
 def fits(R, C, rows, cols, chans, hidden):

time: 40.1 us -> 38.3 us (0.955)
  local copies, waits for them, and re-layouts: 1.87 us -> 0 us
    unnamed x1 -> x0, local copies, waits for them, and re-layouts: 1.87 us -> none
    pallas_call x1 -> x2, Pallas kernels: 38 us -> 38.2 us  [the longest x1 37.4 us: fused(): pl.pallas_call(functools.partial(fused_kernel, R, C), out_shape=pltpu.VME...]
where the time goes in v2:
time: 38.3 us; the launch traced here: 38.2 us
  Pallas kernels  38.2 us (100%)
    pallas_call x1, Pallas kernels, fused(): pl.pallas_call(functools.partial(fused_kernel, R, C), out_shape=pltpu.VME...  37.4 us
    pallas_call x1, Pallas kernels, fused(): pl.pallas_call(write_kernel, out_shape=jax.ShapeDtypeStruct(pair.shape, b...  0.8 us

profile of v2, /device:TPU:0, one launch (start us, length us, event | category | flops | bytes accessed | tf_op | source)
XLA Modules:
  0.0 38.2 jit_solution(4523400665643913684)
XLA Ops:
  0.0 37.4 %shard_map.82.update_ref = bf16[64,4096]{1,0:T(8,128)(2,1)S(1)} custom-call(bf16[64,4096]{1,0:T(8,128)(2,1)} %pair_hbm.1, s32[1,256]{1,0:T(1,128)} %bitcast.4, s32[1,256]{1,0:T(1,128)} %bitcast.5, f32[1,64]{1,0:T(1,128)} %bitcast.6, bf16[64,256]{1,0:T(8,128)(2,1)} %w_proj_hbm.1, bf16[64,64]{1,0:T(8,128)(2,1)} %w_gate_hbm.1, f32[1,64]{1,0:T(1,128)} %bitcast.7, ...), custom_call_target="tpu_custom_call" | custom-call | tf_op jit(solution)/shard_map/pallas_call | solution.py:335
  37.4 0.8 %shard_map.83 = bf16[64,4096]{1,0:T(8,128)(2,1)} custom-call(bf16[64,4096]{1,0:T(8,128)(2,1)S(1)} %shard_map.82.update_ref), custom_call_target="tpu_custom_call" | custom-call | tf_op jit(solution)/shard_map/pallas_call | solution.py:358

commit v3 on v2

--- a/solution.py
+++ b/solution.py
@@ -11,7 +11,7 @@
 NN = (((1,), (0,)), ((), ()))
 EIGHT = 8
 LANES = 128
-CHUNKS = 4
+SIZES = (1, 1, 2, 2, 2)
 WRITE_GRANT = 2**20
 
 
@@ -53,7 +53,8 @@
     depth = R // 2
     team = depth * C
     own = hidden // team
-    per = own // CHUNKS
+    last = len(SIZES) - 1
+    start = [sum(SIZES[:h]) for h in range(len(SIZES))]
     groups = normed.shape[0] // rows
     pairs = groups // 2
     block = EIGHT * chans
@@ -62,6 +63,7 @@
     me = r * C + c
     half_row = r // depth * depth
     seat = r % depth * C + c
+    half = r // depth
 
     def mate(n):
         row = half_row + flipped(r % depth, depth - 1 - n // C, depth)
@@ -70,16 +72,11 @@
     def partner(n):
         return flipped(r, R - 1 - n // C, R), flipped(c, C - 1 - n % C, C)
 
+    def beyond(q, n):
+        return (R - 1) * (1 - half) + q * (2 * half - 1), flipped(c, C - 1 - n, C)
+
     barrier = pltpu.get_barrier_semaphore()
 
-    def greet(n, carry):
-        pr, pc = partner(n)
-        pl.semaphore_signal(
-            barrier, inc=1, device_id={"row": pr, "col": pc}, device_id_type=pl.DeviceIdType.MESH
-        )
-        return carry
-
-    lax.fori_loop(0, ndev - 1, greet, 0)
     loads = [
         pltpu.make_async_copy(source, target, in_sem.at[at])
         for at, (source, target) in enumerate(
@@ -92,9 +89,20 @@
     ]
     for load in loads:
         load.start()
-    for load in loads:
+    def greet(n, carry):
+        pr, pc = partner(n)
+        pl.semaphore_signal(
+            barrier, inc=1, device_id={"row": pr, "col": pc}, device_id_type=pl.DeviceIdType.MESH
+        )
+        return carry
+
+    lax.fori_loop(0, ndev - 1, greet, 0)
+    same = (iota((half_block, half_block), 0) // chans) == (
+        iota((half_block, half_block), 1) // chans
+    )
+    ones = same.astype(f32).astype(bf16)
+    for load in loads[1:]:
         load.wait()
-
     eye = iota((chans, chans), 0) == iota((chans, chans), 1)
     sub_id, lane_in = iota((chans, block), 0), iota((chans, block), 1)
 
@@ -105,10 +113,34 @@
     gain_in = over_lanes(gain_in_ref, lane_in % chans == sub_id)
     gain_out = over_lanes(gain_out_ref, lane_in // EIGHT == sub_id)
 
-    same = (iota((half_block, half_block), 0) // chans) == (
-        iota((half_block, half_block), 1) // chans
-    )
-    ones = same.astype(f32).astype(bf16)
+    count = res_ref.shape[1]
+    alive = (res_ref[...] * present_ref[...]).astype(f32)
+    wide_lanes = groups * rows
+    res_id, lane = iota((count, wide_lanes), 0), iota((count, wide_lanes), 1)
+    group = (lane // rows) % 2 * pairs + lane // LANES
+    is_row = (res_id == r * rows + lane % rows).astype(f32).astype(bf16)
+    is_col = (res_id // EIGHT == c * groups + group).astype(f32).astype(bf16)
+    shape = (max(SIZES) * EIGHT, count)
+    phase = iota(shape, 0) % EIGHT == iota(shape, 1) % EIGHT
+    rows_alive = dot(jnp.broadcast_to(alive, shape).astype(bf16), is_row, NN)
+    masks[...] = rows_alive * dot(jnp.where(phase, alive, 0.0).astype(bf16), is_col, NN)
+
+    stacked = jnp.concatenate([w_proj_ref[...]] * EIGHT, axis=0)
+    out_chans = w_proj_ref.shape[1]
+
+    def weights_of(h):
+        part = SIZES[h] * EIGHT
+        n_rows = team * 4 * part
+        diag = (iota((n_rows, block), 0) % EIGHT) == (iota((n_rows, block), 1) // chans)
+        row_id = iota((n_rows, out_chans), 0)
+        target = row_id // part % 4 * hidden + row_id // (4 * part) * own + row_id % part // EIGHT
+        target = iota((n_rows, out_chans), 1) - target
+        pick = (target == start[h]).astype(f32).astype(bf16)
+        return jnp.where(diag, dot(pick, stacked, NT), 0.0).astype(bf16)
+
+    first_weights = weights_of(0)
+
+    loads[0].wait()
     for h in range(2):
         parts = []
         for qp in range(pairs):
@@ -124,32 +156,11 @@
         y = d * lax.rsqrt(var + 1e-05) * gain_in[:, h * half_block : (h + 1) * half_block]
         normed[:, h * half_block : (h + 1) * half_block] = y.astype(bf16)
 
-    count = res_ref.shape[1]
-    alive = (res_ref[...] * present_ref[...]).astype(f32)
-    wide_lanes = groups * rows
-    res_id, lane = iota((count, wide_lanes), 0), iota((count, wide_lanes), 1)
-    group = (lane // rows) % 2 * pairs + lane // LANES
-    is_row = (res_id == r * rows + lane % rows).astype(f32).astype(bf16)
-    is_col = (res_id // EIGHT == c * groups + group).astype(f32).astype(bf16)
-    shape = (per * EIGHT, count)
-    phase = iota(shape, 0) % EIGHT == iota(shape, 1) % EIGHT
-    rows_alive = dot(jnp.broadcast_to(alive, shape).astype(bf16), is_row, NN)
-    masks[...] = rows_alive * dot(jnp.where(phase, alive, 0.0).astype(bf16), is_col, NN)
-
-    stacked = jnp.concatenate([w_proj_ref[...]] * EIGHT, axis=0)
-    part = per * EIGHT
-    n_rows = team * 4 * part
-    out_chans = w_proj_ref.shape[1]
-    diag = (iota((n_rows, block), 0) % EIGHT) == (iota((n_rows, block), 1) // chans)
-    row_id = iota((n_rows, out_chans), 0)
-    target = row_id // part % 4 * hidden + row_id // (4 * part) * own + row_id % part // EIGHT
-    target = iota((n_rows, out_chans), 1) - target
-
     def project(h):
-        pick = (target == h * per).astype(f32).astype(bf16)
-        weights = jnp.where(diag, dot(pick, stacked, NT), 0.0).astype(bf16)
-        res = dot(weights, normed[...], NT)
-        mask = masks[...]
+        per = SIZES[h]
+        part = per * EIGHT
+        res = dot(weights_of(h) if h > 0 else first_weights, normed[...], NT)
+        mask = masks[:part]
         for dest in range(team):
             for which in range(2):
                 lo = (4 * dest + 2 * which) * part
@@ -163,7 +174,7 @@
                         ],
                         axis=0,
                     )
-                    send1[h, dest, ch, which] = tile.astype(bf16)
+                    send1[dest, start[h] + ch, which] = tile.astype(bf16)
 
     def remote(source, target, ssem, rsem, where):
         return pltpu.make_async_remote_copy(
@@ -171,31 +182,32 @@
             device_id={"row": where[0], "col": where[1]}, device_id_type=pl.DeviceIdType.MESH,
         )
 
-    def copy1(h, n, sending):
+    def span(h):
+        return pl.ds(start[h], SIZES[h])
+
+    def copy1(h, n):
         where = mate(n)
         p = (where[0] - half_row) * C + where[1]
-        at = seat if sending else p
         return remote(
-            send1.at[h, p], recv1.at[h, at], send_sem1.at[0], recv_sem1.at[h], where
-        )
-
-    def copy2(piece, n, sending):
-        where = partner(n)
-        p = where[0] * C + where[1]
-        at = me if sending else p
-        last = CHUNKS - 1
-        key = (lambda d: (piece, d)) if piece < last else (lambda d: (last, d, piece - last))
-        return remote(
-            send2.at[key(p)], recv2.at[key(at)],
-            send_sem2.at[0], recv_sem2.at[piece], where,
-        )
+            send1.at[p, span(h)], recv1.at[seat, span(h)], send_sem1, recv_sem1.at[h], where
+        )
+
+    def views(piece, p):
+        if piece < last:
+            return send2.at[p, span(piece)], recv2.at[me, span(piece)]
+        two = piece - last
+        return send2.at[p, span(last), two], recv2.at[me, span(last), two]
+
+    def copy2(piece, where):
+        source, target = views(piece, where[0] * C + where[1])
+        return remote(source, target, send_sem2, recv_sem2.at[piece], where)
 
     def each(total, body):
         def run(n, carry):
             body(n)
             return carry
 
-        lax.fori_loop(0, total - 1, run, 0)
+        lax.fori_loop(0, total, run, 0)
 
     gate_rows = jnp.concatenate([w_gate_ref[...]] * (half_block // chans), axis=0)
     spread = ((iota((chans, block), 1) % chans) == iota((chans, block), 0)).astype(f32).astype(bf16)
@@ -204,11 +216,6 @@
     def output_gate(h):
         cols = slice(h * half_block, (h + 1) * half_block)
         gate[:, cols] = jax.nn.sigmoid(dot(normed[:, cols], w_gate4, NN))
-
-    own1 = [
-        pltpu.make_async_copy(send1.at[h, seat], recv1.at[h, seat], recv_sem1.at[h])
-        for h in range(CHUNKS)
-    ]
 
     def landed(ref, sem):
         pltpu.make_async_copy(ref, ref, sem).wait()
@@ -220,14 +227,14 @@
 
     sub = pairs * EIGHT
 
-    def multiply(h, ch):
+    def multiply(ch):
         full = []
         for which in range(2):
             by_parity = [[], []]
             for rp in range(depth // 2):
                 one, two = (
                     jnp.concatenate(
-                        [recv1[h, (2 * rp + e) * C + cc, ch, which] for cc in range(C)], axis=0
+                        [recv1[(2 * rp + e) * C + cc, ch, which] for cc in range(C)], axis=0
                     ).astype(f32)
                     for e in range(2)
                 )
@@ -245,51 +252,46 @@
                 for cc in range(C):
                     for two in range(2):
                         lo = cc * sub + two * (sub // 2)
-                        send2[h, (2 * rp + e) * C + cc, two, ch] = tile[lo : lo + sub // 2]
-
-    def own2(piece):
-        if piece < CHUNKS - 1:
-            source, target = send2.at[piece, me], recv2.at[piece, me]
-        else:
-            half = piece - CHUNKS + 1
-            source, target = send2.at[CHUNKS - 1, me, half], recv2.at[CHUNKS - 1, me, half]
-        return pltpu.make_async_copy(source, target, recv_sem2.at[piece])
+                        send2[(2 * rp + e) * C + cc, ch, two] = tile[lo : lo + sub // 2]
+
+    def begin(h):
+        each(team - 1, lambda n: copy1(h, n).start())
+        pltpu.make_async_copy(
+            send1.at[seat, span(h)], recv1.at[seat, span(h)], recv_sem1.at[h]
+        ).start()
 
     def answer(h):
-        landed(recv1.at[h], recv_sem1.at[h])
-        for ch in range(per):
-            multiply(h, ch)
-        for piece in (h,) if h < CHUNKS - 1 else (h, h + 1):
-            each(ndev, lambda n, piece=piece: copy2(piece, n, True).start())
-            own2(piece).start()
-
-    for h in range(CHUNKS):
+        landed(recv1.at[:, span(h)], recv_sem1.at[h])
+        for ch in range(SIZES[h]):
+            multiply(start[h] + ch)
+        pieces = (h,) if h < last else (h, h + 1)
+        for q in range(depth):
+            for piece in pieces:
+                each(C, lambda n, q=q, piece=piece: copy2(piece, beyond(q, n)).start())
+        for piece in pieces:
+            each(team - 1, lambda n, piece=piece: copy2(piece, partner(n + team)).start())
+            source, target = views(piece, me)
+            pltpu.make_async_copy(source, target, recv_sem2.at[piece]).start()
+
+    for h in range(len(SIZES)):
         project(h)
         if h == 0:
             pl.semaphore_wait(barrier, ndev - 1)
         if h in (1, 2):
             output_gate(h - 1)
-        each(team, lambda n, h=h: copy1(h, n, True).start())
-        own1[h].start()
+        begin(h)
         if h >= 2:
             answer(h - 2)
-    for h in range(max(CHUNKS - 2, 0), CHUNKS):
+    for h in range(len(SIZES) - 2, len(SIZES)):
         answer(h)
-    for h in range(max(CHUNKS, 1), 3):
-        output_gate(h - 1)
     wide[...] = jnp.where(diag_out, dot(pick_out, tiled, NN), 0.0).astype(bf16)
 
-    for piece in range(CHUNKS - 1):
-        landed(recv2.at[piece], recv_sem2.at[piece])
+    for piece in range(last):
+        landed(recv2.at[:, span(piece)], recv_sem2.at[piece])
     for two in range(pairs // 2):
-        landed(recv2.at[CHUNKS - 1, :, two], recv_sem2.at[CHUNKS - 1 + two])
-        t = jnp.concatenate(
-            [
-                (recv2[h, :team, two].astype(f32) + recv2[h, team:, two].astype(f32))[:, None]
-                for h in range(CHUNKS)
-            ],
-            axis=1,
-        ).reshape(hidden, 16, LANES)
+        landed(recv2.at[:, span(last), two], recv_sem2.at[last + two])
+        t = recv2[:team, :, two].astype(f32) + recv2[team:, :, two].astype(f32)
+        t = t.reshape(hidden, 16, LANES)
         mean = jnp.sum(t, axis=0, keepdims=True) * (1.0 / hidden)
         d = t - mean
         var = jnp.sum(d * d, axis=0, keepdims=True) * (1.0 / hidden)
@@ -304,8 +306,8 @@
                 val = g * res[par * rows : (par + 1) * rows]
                 lo = (par * pairs + qp) * block
                 out_ref[:, lo : lo + block] = val.astype(bf16)
-    landed(send1.at[:, pl.ds(0, team - 1)], send_sem1.at[0])
-    landed(send2.at[:, pl.ds(0, ndev - 1)], send_sem2.at[0])
+    landed(send1.at[pl.ds(0, team - 1)], send_sem1)
+    landed(send2.at[pl.ds(0, ndev - 1)], send_sem2)
 
 
 def write_kernel(update_ref, out_hbm, sem):
@@ -323,8 +325,7 @@
     pairs = groups // 2
     ndev = R * C
     team = ndev // 2
-    own = hidden // team
-    per = own // CHUNKS
+    own = sum(SIZES)
     bf16 = jnp.bfloat16
     anywhere = pl.BlockSpec(memory_space=pl.ANY)
     operands = (
@@ -342,15 +343,15 @@
             pltpu.VMEM((groups * rows, EIGHT * chans), bf16),
             pltpu.VMEM((groups * rows, EIGHT * chans), jnp.float32),
             pltpu.VMEM((hidden * EIGHT, EIGHT * chans), bf16),
-            pltpu.VMEM((per * EIGHT, groups * rows), jnp.float32),
-            pltpu.VMEM((CHUNKS, team, per, 2, sub, LANES), bf16),
-            pltpu.VMEM((CHUNKS, team, per, 2, sub, LANES), bf16),
-            pltpu.VMEM((CHUNKS, ndev, 2, per, sub // 2, LANES), bf16),
-            pltpu.VMEM((CHUNKS, ndev, 2, per, sub // 2, LANES), bf16),
-            pltpu.SemaphoreType.DMA((1,)),
-            pltpu.SemaphoreType.DMA((CHUNKS,)),
-            pltpu.SemaphoreType.DMA((1,)),
-            pltpu.SemaphoreType.DMA((CHUNKS + 1,)),
+            pltpu.VMEM((max(SIZES) * EIGHT, groups * rows), jnp.float32),
+            pltpu.VMEM((team, own, 2, sub, LANES), bf16),
+            pltpu.VMEM((team, own, 2, sub, LANES), bf16),
+            pltpu.VMEM((ndev, own, 2, sub // 2, LANES), bf16),
+            pltpu.VMEM((ndev, own, 2, sub // 2, LANES), bf16),
+            pltpu.SemaphoreType.DMA,
+            pltpu.SemaphoreType.DMA((len(SIZES),)),
+            pltpu.SemaphoreType.DMA,
+            pltpu.SemaphoreType.DMA((len(SIZES) + 1,)),
             pltpu.SemaphoreType.DMA((len(operands),)),
         ],
         compiler_params=pltpu.CompilerParams(collective_id=0, has_side_effects=True),
@@ -373,7 +374,8 @@
         and R % 4 == 0
         and rows == cols == LANES // 2
         and chans == hidden == LANES // 2
-        and hidden % (R * C // 2 * CHUNKS) == 0
+        and R // 2 == 2
+        and hidden == R * C // 2 * sum(SIZES)
     )
 
 

time: 38.3 us -> 37.6 us (0.982)
  Pallas kernels: 38.2 us -> 37.4 us
    pallas_call x1, Pallas kernels: 37.4 us -> 36.6 us  [fused(): pl.pallas_call(functools.partial(fused_kernel, R, C), out_shape=pltpu.VME...]
where the time goes in v3:
time: 37.6 us; the launch traced here: 37.5 us
  Pallas kernels  37.4 us (99%)
    pallas_call x1, Pallas kernels, fused(): pl.pallas_call(functools.partial(fused_kernel, R, C), out_shape=pltpu.VME...  36.6 us
    pallas_call x1, Pallas kernels, fused(): pl.pallas_call(write_kernel, out_shape=jax.ShapeDtypeStruct(pair.shape, b...  0.8 us

profile of v3, /device:TPU:0, one launch (start us, length us, event | category | flops | bytes accessed | tf_op | source)
XLA Modules:
  0.0 37.5 jit_solution(2745908915868817950)
XLA Ops:
  0.0 36.6 %shard_map.82.update_ref = bf16[64,4096]{1,0:T(8,128)(2,1)S(1)} custom-call(bf16[64,4096]{1,0:T(8,128)(2,1)} %pair_hbm.1, s32[1,256]{1,0:T(1,128)} %bitcast.4, s32[1,256]{1,0:T(1,128)} %bitcast.5, f32[1,64]{1,0:T(1,128)} %bitcast.6, bf16[64,256]{1,0:T(8,128)(2,1)} %w_proj_hbm.1, bf16[64,64]{1,0:T(8,128)(2,1)} %w_gate_hbm.1, f32[1,64]{1,0:T(1,128)} %bitcast.7, ...), custom_call_target="tpu_custom_call" | custom-call | tf_op jit(solution)/shard_map/pallas_call | solution.py:336
  36.7 0.8 %shard_map.83 = bf16[64,4096]{1,0:T(8,128)(2,1)} custom-call(bf16[64,4096]{1,0:T(8,128)(2,1)S(1)} %shard_map.82.update_ref), custom_call_target="tpu_custom_call" | custom-call | tf_op jit(solution)/shard_map/pallas_call | solution.py:359

commit v4 on v3

--- a/solution.py
+++ b/solution.py
@@ -42,8 +42,8 @@
 def fused_kernel(
     R, C, pair_hbm, res_hbm, present_hbm, gain_in_hbm, w_proj_hbm, w_gate_hbm, gain_out_hbm,
     w_out_hbm, out_ref, pair_ref, res_ref, present_ref, gain_in_ref, w_proj_ref, w_gate_ref,
-    gain_out_ref, w_out_ref, normed, gate, wide, masks, send1, recv1, send2, recv2,
-    send_sem1, recv_sem1, send_sem2, recv_sem2, in_sem,
+    gain_out_ref, w_out_ref, normed, gate, wide, masks, send1, recv1, send2, recv2, joined,
+    send_sem1, recv_sem1, send_sem2, recv_sem2, join_sem, in_sem,
 ):
     f32, bf16 = jnp.float32, jnp.bfloat16
     rows = pair_ref.shape[0]
@@ -54,6 +54,7 @@
     team = depth * C
     own = hidden // team
     last = len(SIZES) - 1
+    folds = last
     start = [sum(SIZES[:h]) for h in range(len(SIZES))]
     groups = normed.shape[0] // rows
     pairs = groups // 2
@@ -64,6 +65,7 @@
     half_row = r // depth * depth
     seat = r % depth * C + c
     half = r // depth
+    middle = (r % depth + half) % 2
 
     def mate(n):
         row = half_row + flipped(r % depth, depth - 1 - n // C, depth)
@@ -139,6 +141,13 @@
         return jnp.where(diag, dot(pick, stacked, NT), 0.0).astype(bf16)
 
     first_weights = weights_of(0)
+
+    @pl.when(middle == 0)
+    def _():
+        for cc in range(C):
+            recv2[(R - 1 - r) * C + cc, : start[folds]] = jnp.zeros(
+                (start[folds],) + recv2.shape[2:], bf16
+            )
 
     loads[0].wait()
     for h in range(2):
@@ -254,6 +263,30 @@
                         lo = cc * sub + two * (sub // 2)
                         send2[(2 * rp + e) * C + cc, ch, two] = tile[lo : lo + sub // 2]
 
+    def piece_of(ref, row, piece):
+        if piece < last:
+            return ref.at[row, span(piece)]
+        return ref.at[row, span(last), piece - last]
+
+    def copy_join(piece, n):
+        row, col = beyond(0, n)
+        return remote(
+            piece_of(send2, row * C + col, piece), piece_of(joined, col, piece),
+            send_sem2, join_sem.at[piece], (beyond(1, n)[0], c),
+        )
+
+    def join(piece):
+        chans_of = slice(start[min(piece, last)], start[min(piece, last)] + SIZES[min(piece, last)])
+        two = slice(0, 2) if piece < last else slice(piece - last, piece - last + 1)
+        every = joined.at[:, span(piece)] if piece < last else joined.at[:, span(last), piece - last]
+        landed(every, join_sem.at[piece])
+        row = flipped(r, 1, R)
+        for cc in range(C):
+            both = send2[row * C + cc, chans_of, two].astype(f32)
+            both = both + joined[cc, chans_of, two].astype(f32)
+            send2[row * C + cc, chans_of, two] = both.astype(bf16)
+        each(C, lambda n: copy2(piece, partner(n + team)).start())
+
     def begin(h):
         each(team - 1, lambda n: copy1(h, n).start())
         pltpu.make_async_copy(
@@ -265,11 +298,30 @@
         for ch in range(SIZES[h]):
             multiply(start[h] + ch)
         pieces = (h,) if h < last else (h, h + 1)
-        for q in range(depth):
+        if h < folds:
+
+            @pl.when(middle == 1)
+            def _():
+                each(C, lambda n: copy2(h, beyond(0, n)).start())
+
+            @pl.when(middle == 0)
+            def _():
+                each(C, lambda n: copy_join(h, n).start())
+
+            each(C, lambda n: copy2(h, beyond(1, n)).start())
+
+            @pl.when(middle == 0)
+            def _():
+                each(C, lambda n: copy2(h, partner(n + team)).start())
+
+        else:
+            for q in range(depth):
+                for piece in pieces:
+                    each(C, lambda n, q=q, piece=piece: copy2(piece, beyond(q, n)).start())
             for piece in pieces:
-                each(C, lambda n, q=q, piece=piece: copy2(piece, beyond(q, n)).start())
+                each(C, lambda n, piece=piece: copy2(piece, partner(n + team)).start())
         for piece in pieces:
-            each(team - 1, lambda n, piece=piece: copy2(piece, partner(n + team)).start())
+            each(C - 1, lambda n, piece=piece: copy2(piece, partner(n + team + C)).start())
             source, target = views(piece, me)
             pltpu.make_async_copy(source, target, recv_sem2.at[piece]).start()
 
@@ -286,10 +338,25 @@
         answer(h)
     wide[...] = jnp.where(diag_out, dot(pick_out, tiled, NN), 0.0).astype(bf16)
 
+    @pl.when(middle == 1)
+    def _():
+        for piece in range(folds):
+            join(piece)
+
+    def arrived(piece):
+        if piece >= folds:
+            landed(piece_of(recv2, slice(None), piece), recv_sem2.at[piece])
+            return
+        for kind, slots in ((0, pl.ds(0, ndev - C)), (1, pl.ds(0, ndev))):
+
+            @pl.when(middle == kind)
+            def _():
+                landed(piece_of(recv2, slots, piece), recv_sem2.at[piece])
+
     for piece in range(last):
-        landed(recv2.at[:, span(piece)], recv_sem2.at[piece])
+        arrived(piece)
     for two in range(pairs // 2):
-        landed(recv2.at[:, span(last), two], recv_sem2.at[last + two])
+        arrived(last + two)
         t = recv2[:team, :, two].astype(f32) + recv2[team:, :, two].astype(f32)
         t = t.reshape(hidden, 16, LANES)
         mean = jnp.sum(t, axis=0, keepdims=True) * (1.0 / hidden)
@@ -348,10 +415,12 @@
             pltpu.VMEM((team, own, 2, sub, LANES), bf16),
             pltpu.VMEM((ndev, own, 2, sub // 2, LANES), bf16),
             pltpu.VMEM((ndev, own, 2, sub // 2, LANES), bf16),
+            pltpu.VMEM((C, own, 2, sub // 2, LANES), bf16),
             pltpu.SemaphoreType.DMA,
             pltpu.SemaphoreType.DMA((len(SIZES),)),
             pltpu.SemaphoreType.DMA,
             pltpu.SemaphoreType.DMA((len(SIZES) + 1,)),
+            pltpu.SemaphoreType.DMA((len(SIZES),)),
             pltpu.SemaphoreType.DMA((len(operands),)),
         ],
         compiler_params=pltpu.CompilerParams(collective_id=0, has_side_effects=True),

time: 37.6 us -> 36.7 us (0.976)
  Pallas kernels: 37.4 us -> 36.6 us
    pallas_call x1, Pallas kernels: 36.6 us -> 35.7 us  [fused(): pl.pallas_call(functools.partial(fused_kernel, R, C), out_shape=pltpu.VME...]
where the time goes in v4:
time: 36.7 us; the launch traced here: 36.6 us
  Pallas kernels  36.6 us (100%)
    pallas_call x1, Pallas kernels, fused(): pl.pallas_call(functools.partial(fused_kernel, R, C), out_shape=pltpu.VME...  35.7 us
    pallas_call x1, Pallas kernels, fused(): pl.pallas_call(write_kernel, out_shape=jax.ShapeDtypeStruct(pair.shape, b...  0.8 us

profile of v4, /device:TPU:0, one launch (start us, length us, event | category | flops | bytes accessed | tf_op | source)
XLA Modules:
  0.0 36.6 jit_solution(2559969223835054831)
XLA Ops:
  0.0 35.7 %shard_map.82.update_ref = bf16[64,4096]{1,0:T(8,128)(2,1)S(1)} custom-call(bf16[64,4096]{1,0:T(8,128)(2,1)} %pair_hbm.1, s32[1,256]{1,0:T(1,128)} %bitcast.4, s32[1,256]{1,0:T(1,128)} %bitcast.5, f32[1,64]{1,0:T(1,128)} %bitcast.6, bf16[64,256]{1,0:T(8,128)(2,1)} %w_proj_hbm.1, bf16[64,64]{1,0:T(8,128)(2,1)} %w_gate_hbm.1, f32[1,64]{1,0:T(1,128)} %bitcast.7, ...), custom_call_target="tpu_custom_call" | custom-call | tf_op jit(solution)/shard_map/pallas_call | solution.py:403
  35.8 0.8 %shard_map.83 = bf16[64,4096]{1,0:T(8,128)(2,1)} custom-call(bf16[64,4096]{1,0:T(8,128)(2,1)S(1)} %shard_map.82.update_ref), custom_call_target="tpu_custom_call" | custom-call | tf_op jit(solution)/shard_map/pallas_call | solution.py:428
